TPU v7x, 32 devices: a whole 2x2x4 slice. The times are simulated.
32 devices in a mesh: group: 2 (over x), sec: 16 (over z, y, core).
Axes of the slice: x: 2, y: 2, z: 4, core: 2. Of those that a mesh axis runs over, the one named last changes fastest.
Arguments:
- residual: bfloat16 [4096, 256], P('sec', 'group'), parts along dimension 1, may hold values from -80 to 80
- queries: bfloat16 [256, 4096], P(('group', 'sec')), parts along dimension 0, may hold values from -200 to 200
- new_keys: bfloat16 [256, 512], P(('group', 'sec')), parts along dimension 0, may hold values from -7 to 7
- new_values: bfloat16 [256, 512], P(('group', 'sec')), parts along dimension 0, may hold values from -6 to 6
- cache_keys: bfloat16 [256, 128, 512], P(('group', 'sec')), parts along dimension 0, may hold values from -6 to 6
- cache_values: bfloat16 [256, 128, 512], P(('group', 'sec')), parts along dimension 0, may hold values from -6 to 6
- cache_lengths: int32 [256], P(('group', 'sec')), parts along dimension 0, may hold values from 1 to 128, 4096 in all
- slot_of_row: int32 [256], P('group'), parts along dimension 0, may hold values from 0 to 127, each once
- out_weight: bfloat16 [4096, 4096], P('sec'), may hold values from -0.09375 to 0.09375
- norm_gain: float32 [4096], replicated, may hold values from 0.1 to 1.9
- gate_weight: bfloat16 [28672, 4096], P('sec'), may hold values from -0.09375 to 0.09375
- up_weight: bfloat16 [28672, 4096], P('sec'), may hold values from -0.09375 to 0.09375
- down_weight: bfloat16 [28672, 4096], P('sec'), may hold values from -0.046875 to 0.046875
Outputs:
- layer_out: bfloat16 [4096, 256], P('sec', 'group'), parts along dimension 1
There are 2 independent parts, one for each index of `group`. A program takes and returns all parts, laid end to end along the dimension named above; an argument that names none is the same for every part. Nothing has to cross between parts.
Inputs may be any that keep to these rules, and one draw needn't show every extreme that they name: `slot_of_row`: each of 0 to 127 once. `cache_lengths`: the lengths sum to 4096 and the largest is exactly 128.
All inputs are finite; a program needn't handle non-finite values. No bound on the sum of `cache_lengths` on one device may be relied on, other than what follows from the above.
Results may differ from a plain program's by a relative error of at most 0.0095.
Values may be sent and summed in bfloat16 or wider, within the bound.
No kernel may reach another device: no remote copies, remote signals or barrier semaphores. Data moves between devices by JAX's collectives and lax.ppermute only.
A program may use at most 128 MiB of HBM per device.

v0:
```python
import math

import jax
import jax.numpy as jnp
from jax import lax
from jax.sharding import PartitionSpec as P

H = 32
KVH = 4
HD = 128


EPSILON = 1e-05


def attend(queries, new_keys, new_values, cache_keys, cache_values, cache_lengths):
    row_count = queries.shape[0]
    positions_total = cache_keys.shape[1]
    grouped = H // KVH
    scaling = 1.0 / math.sqrt(HD)
    query_heads = queries.reshape(row_count, KVH, grouped, HD)
    cached_keys = cache_keys.reshape(row_count, positions_total, KVH, HD)
    cached_values = cache_values.reshape(row_count, positions_total, KVH, HD)
    fresh_keys = new_keys.reshape(row_count, KVH, HD)
    scores = (
        jnp.einsum("rkgd,rpkd->rkgp", query_heads, cached_keys, preferred_element_type=jnp.float32)
        * scaling
    )
    fresh_score = (
        jnp.einsum("rkgd,rkd->rkg", query_heads, fresh_keys, preferred_element_type=jnp.float32)
        * scaling
    )
    positions = lax.broadcasted_iota(jnp.int32, scores.shape, 3)
    usable = positions < cache_lengths[:, None, None, None]
    highest = jnp.maximum(jnp.max(jnp.where(usable, scores, -jnp.inf), axis=3), fresh_score)
    weights = jnp.where(usable, jnp.exp(scores - highest[..., None]), 0.0)
    fresh_weight = jnp.exp(fresh_score - highest)
    summed = jnp.sum(weights, axis=3) + fresh_weight
    weights = (weights / summed[..., None]).astype(jnp.bfloat16)
    fresh_weight = (fresh_weight / summed).astype(jnp.bfloat16)
    mixture = jnp.einsum(
        "rkgp,rpkd->rkgd", weights, cached_values, preferred_element_type=jnp.float32
    )
    mixture = mixture + fresh_weight.astype(jnp.float32)[..., None] * new_values.astype(
        jnp.float32
    ).reshape(row_count, KVH, 1, HD)
    return mixture.reshape(row_count, H * HD).astype(jnp.bfloat16)


def on_device(
    residual,
    queries,
    new_keys,
    new_values,
    cache_keys,
    cache_values,
    cache_lengths,
    slot_of_row,
    out_weight,
    norm_gain,
    gate_weight,
    up_weight,
    down_weight,
):
    attended = attend(queries, new_keys, new_values, cache_keys, cache_values, cache_lengths)
    local_rows = attended.shape[0]
    devices = lax.axis_size("sec")
    bounds = (0, local_rows)
    inverse = jnp.argsort(slot_of_row)
    lower_row, upper_row = bounds
    batch_rows = upper_row - lower_row
    slot_ids = (
        jnp.arange(devices, dtype=jnp.int32)[:, None] * local_rows
        + lower_row
        + jnp.arange(batch_rows, dtype=jnp.int32)[None, :]
    ).reshape(-1)
    position_of = jnp.argsort(slot_ids)
    residual_part = jnp.take(residual, inverse[slot_ids], axis=1)
    branch = lax.dot_general(
        out_weight,
        lax.all_gather(attended, "sec", axis=0, tiled=True),
        (((1,), (1,)), ((), ())),
        preferred_element_type=jnp.float32,
    )
    stream = (residual_part.astype(jnp.float32) + branch).astype(jnp.bfloat16)
    gathered = lax.all_gather(stream, "sec", axis=0, tiled=True)
    widened_all = gathered.astype(jnp.float32)
    mean_square = jnp.mean(widened_all * widened_all, axis=0)
    normed_all = (
        widened_all * lax.rsqrt(mean_square + EPSILON)[None, :] * norm_gain[:, None]
    ).astype(jnp.bfloat16)
    gate_sum = jnp.dot(gate_weight, normed_all, preferred_element_type=jnp.float32)
    up_sum = jnp.dot(up_weight, normed_all, preferred_element_type=jnp.float32)
    hidden = (jax.nn.silu(gate_sum) * up_sum).astype(jnp.bfloat16)
    lowered = lax.psum_scatter(
        lax.dot_general(
            down_weight, hidden, (((0,), (0,)), ((), ())), preferred_element_type=jnp.float32
        ),
        "sec",
        scatter_dimension=0,
        tiled=True,
    )
    outputs = (stream.astype(jnp.float32) + lowered).astype(jnp.bfloat16)
    return jnp.take(outputs, position_of[slot_of_row], axis=1)


def solution(mesh):
    in_specs = (
        P("sec", "group"),
        P(("group", "sec"), None),
        P(("group", "sec"), None),
        P(("group", "sec"), None),
        P(("group", "sec"), None, None),
        P(("group", "sec"), None, None),
        P(("group", "sec")),
        P("group"),
        P("sec", None),
        P(),
        P("sec", None),
        P("sec", None),
        P("sec", None),
    )
    out_specs = P("sec", "group")
    return jax.shard_map(
        on_device, mesh=mesh, in_specs=in_specs, out_specs=out_specs, check_vma=False
    )
```

profile of v0, /device:TPU:0, one launch (start us, length us, event | category | flops | bytes accessed | tf_op | source)
XLA Modules:
  0.0 191.9 jit_solution(10638976317520496633)
XLA Ops:
  6.5 0.0 copy-start
  6.5 0.0 copy-start.3
  6.5 0.0 copy-start.5
  6.5 0.0 all-gather.3.cloned.1.call-start
  6.5 0.9 bitcast_convert_fusion
  7.4 1.0 fusion.22
  8.4 1.9 %select_reduce_fusion = (f32[8,4,8]{2,1,0:T(4,128)S(1)}, f32[8,4,8,128]{3,2,1,0:T(8,128)S(1)}) fusion(s32[8]{0:T(128)} %param.21, bf16[8,4,8,128]{3,0,2,1:T(8,128)(2,1)} %bitcast.62, bf16[8,128,512]{2,1,0:T(8,128)(2,1)} %param.19), kind=kOutput, calls=%fused_computation.29 | convolution fusion | flops 8519424 | bytes 1246240 | tf_op jit(solution)/shard_map/rkgd,rpkd->rkgp/dot_general | solution.py:26
  10.4 0.9 fusion.17
  11.3 1.7 fusion.8
  13.0 0.7 copy.50
  13.6 0.0 all-gather.3.cloned.1.call-update
  13.7 0.0 all-gather.5.cloned.1.call-start
  13.7 0.1 iota_add_fusion
  13.8 0.1 add.83
  13.9 0.0 copy-done.3
  13.9 0.1 copy.20
  14.0 0.0 copy-done.5
  14.0 2.6 %sort.31 = (s32[128]{0:T(128)}, s32[128]{0:T(128)S(1)}) sort(s32[128]{0:T(128)S(1)} %copy-done.5, s32[128]{0:T(128)S(1)} %iota.23), dimensions={0}, to_apply=%region_0.1 | sort | flops 896 | bytes 2048 | tf_op jit(solution)/shard_map/jit(argsort)/sort | solution.py:69
  16.7 1.2 gather_fusion
  17.9 0.8 gather_fusion.2
  18.8 0.0 copy-start.4
  18.8 35.7 %all-gather.3.cloned.1.call-done = bf16[128,4096]{1,0:T(8,128)(2,1)} async-done(((bf16[8,4096]{1,0:T(8,128)(2,1)}), bf16[128,4096]{1,0:T(8,128)(2,1)}) %all-gather.3.cloned.1.call-update) | async-done | bytes 1048592 | tf_op jit(solution)/shard_map/all_gather | solution.py:81
  54.4 0.0 copy-done
  54.5 2.7 %fusion.7 = bf16[256,128]{0,1:T(8,128)(2,1)} fusion(bf16[128,4096]{1,0:T(8,128)(2,1)} %all-gather.3.cloned.1.call-done, bf16[256,4096]{1,0:T(8,128)(2,1)S(1)} %copy-done, bf16[128,256]{1,0:T(8,128)(2,1)S(1)} %gather_fusion.2, pred[128]{0:T(512)(128)(4,1)S(1)} %compare_and_fusion.1), kind=kOutput, calls=%fused_computation.19 | convolution fusion | flops 268566528 | bytes 3276928 | tf_op jit(solution)/shard_map/dot_general | solution.py:79
  57.1 0.0 all-gather.5.cloned.1.call-update
  57.2 0.0 reduce-scatter.2.cloned.1.call-start
  57.2 35.7 %all-gather.5.cloned.1.call-done = bf16[4096,128]{0,1:T(8,128)(2,1)} async-done(((bf16[256,128]{0,1:T(8,128)(2,1)}), bf16[4096,128]{0,1:T(8,128)(2,1)}) %all-gather.5.cloned.1.call-update) | async-done | bytes 1048592 | tf_op jit(solution)/shard_map/all_gather | solution.py:86
  92.9 1.5 fusion.2
  94.5 0.0 copy-done.4
  94.5 0.0 copy-start.1
  94.5 11.5 %convolution_bitcast_fusion.2 = f32[1792,128]{0,1:T(8,128)} fusion(bf16[1792,4096]{1,0:T(8,128)(2,1)} %param.25, bf16[4096,128]{0,1:T(8,128)(2,1)} %all-gather.5.cloned.1.call-done, f32[4096]{0:T(1024)S(1)} %copy-done.4, f32[128]{0:T(128)S(1)} %add_rsqrt_fusion), kind=kOutput, calls=%fused_computation.9 | convolution fusion | flops 1881145344 | bytes 16663040 | tf_op jit(solution)/shard_map/dot_general | solution.py:92
  106.0 0.0 copy-done.1
  106.0 15.1 %convolution_bitcast_fusion = f32[4096,128]{0,1:T(8,128)} fusion(bf16[1792,4096]{1,0:T(8,128)(2,1)} %param.27, bf16[1792,4096]{1,0:T(8,128)(2,1)} %param.26, f32[1792,128]{0,1:T(8,128)} %convolution_bitcast_fusion.2, bf16[4096,128]{0,1:T(8,128)(2,1)S(1)} %copy-done.1, f32[4096]{0:T(1024)S(1)} %copy-done.4, f32[128]{0:T(128)S(1)} %add_rsqrt_fusion), kind=kOutput, calls=%fused_computation.4 | convolution fusion | flops 3761569792 | bytes 33440256 | tf_op jit(solution)/shard_map/dot_general | solution.py:96
  121.1 0.0 copy-start.2
  121.1 0.0 reduce-scatter.2.cloned.1.call-update
  121.1 0.1 add.92
  121.2 2.6 %sort.32 = (s32[128]{0:T(128)}, s32[128]{0:T(128)S(1)}) sort(s32[128]{0:T(128)S(1)} %add.92, s32[128]{0:T(128)S(1)} %iota.26), dimensions={0}, to_apply=%region_5.7 | sort | flops 896 | bytes 2048 | tf_op jit(solution)/shard_map/jit(argsort)/sort | solution.py:77
  123.8 1.2 gather_fusion.1
  125.1 57.6 %reduce-scatter.2.cloned.1.call-done = f32[256,128]{0,1:T(8,128)} async-done(((f32[4096,128]{0,1:T(8,128)}), f32[256,128]{0,1:T(8,128)}) %reduce-scatter.2.cloned.1.call-update) | async-done | bytes 131088 | tf_op jit(solution)/shard_map/reduce_scatter | solution.py:95
  182.7 0.0 copy-done.2
  182.7 0.9 add_convert_fusion
  183.7 0.8 gather_fusion.3
  184.5 0.1 select_bitcast_fusion
  184.6 0.7 copy.25
  (17 shorter events, 0.1 us)
Async XLA Ops:
  6.5 47.9 %copy-start = (bf16[256,4096]{1,0:T(8,128)(2,1)S(1)}, bf16[256,4096]{1,0:T(8,128)(2,1)}, u32[]{:S(2)}) copy-start(bf16[256,4096]{1,0:T(8,128)(2,1)} %param.23) | copy-start | bytes 6291460
  6.5 7.4 %copy-start.3 = (bf16[256,128]{1,0:T(8,128)(2,1)S(1)}, bf16[256,128]{1,0:T(8,128)(2,1)}, u32[]{:S(2)}) copy-start(bf16[256,128]{1,0:T(8,128)(2,1)} %param.15) | copy-start | bytes 196612
  6.5 7.5 %copy-start.5 = (s32[128]{0:T(128)S(1)}, s32[128]{0:T(128)}, u32[]{:S(2)}) copy-start(s32[128]{0:T(128)} %param.22) | copy-start | bytes 1540
  6.5 47.9 %all-gather.3.cloned.1.call-start = ((), (), s32[]{:S(2)}) async-start(), calls=%async_computation.1 | async-start | bytes 1114112 | tf_op jit(solution)/shard_map/all_gather | solution.py:81
  13.7 79.3 %all-gather.5.cloned.1.call-start = ((), (), s32[]{:S(2)}) async-start(), calls=%async_computation.2 | async-start | bytes 1114112 | tf_op jit(solution)/shard_map/all_gather | solution.py:86
  18.8 75.7 %copy-start.4 = (f32[4096]{0:T(1024)S(1)}, f32[4096]{0:T(1024)}, u32[]{:S(2)}) copy-start(f32[4096]{0:T(1024)} %param.24) | copy-start | bytes 49156
  57.2 125.6 %reduce-scatter.2.cloned.1.call-start = ((), (), s32[]{:S(2)}) async-start(), calls=%async_computation.3 | async-start | bytes 2228224 | tf_op jit(solution)/shard_map/reduce_scatter | solution.py:95
  94.5 11.5 %copy-start.1 = (bf16[4096,128]{0,1:T(8,128)(2,1)S(1)}, bf16[4096,128]{0,1:T(8,128)(2,1)}, u32[]{:S(2)}) copy-start(bf16[4096,128]{0,1:T(8,128)(2,1)} %all-gather.5.cloned.1.call-done) | copy-start | bytes 3145732
  121.1 61.7 %copy-start.2 = (bf16[256,128]{0,1:T(8,128)(2,1)S(1)}, bf16[256,128]{0,1:T(8,128)(2,1)}, u32[]{:S(2)}) copy-start(bf16[256,128]{0,1:T(8,128)(2,1)} %fusion.7) | copy-start | bytes 196612
Sparse Core Ops, SparseCore 0:
  13.8 40.6 all-gather.2
  57.3 35.6 all-gather.4
  121.2 61.4 reduce-scatter.1
where the time goes:
time: 192 us
  waiting for transfers between devices  129 us (67%)
  matrix products  33.9 us (18%)
  between operations  13.3 us (7%)
  other arithmetic  9.64 us (5%)
  local copies, waits for them, and re-layouts  5.86 us (3%)
    reduce_scatter x1, waiting for transfers between devices, on_device(): lax.psum_scatter(lax.dot_general(down_weight, hidden, (((0,), (0,)), ((),...  57.6 us
    all_gather x1, waiting for transfers between devices, on_device(): gathered = lax.all_gather(stream, 'sec', axis=0, tiled=True)  35.7 us
    all_gather x1, waiting for transfers between devices, on_device(): lax.all_gather(attended, 'sec', axis=0, tiled=True)  35.7 us
    dot_general x1, matrix products, on_device(): lax.dot_general(down_weight, hidden, (((0,), (0,)), ((), ())), preferred_...  15.1 us
    dot_general x1, matrix products, on_device(): jnp.dot(gate_weight, normed_all, preferred_element_type=jnp.float32)  11.5 us
  transfers between devices with their start and end apart: 3, of which 3 were waited for; matrix products, arithmetic and copies ran while one was open for 5% of the time, Pallas kernels for 0%

commit v1 on v0

v1 whole, which is shorter than its diff:
```python
import functools
import math

import jax
import jax.numpy as jnp
from jax import lax
from jax.experimental import pallas as pl
from jax.experimental.pallas import tpu as pltpu
from jax.sharding import PartitionSpec as P


H = 32
KVH = 4
HD = 128

EPSILON = 1e-05

F32 = jnp.float32
BF16 = jnp.bfloat16
NT = (((1,), (1,)), ((), ()))
MIB = 1 << 20


SMEM = pl.BlockSpec(memory_space=pltpu.SMEM)
VMEM = pl.BlockSpec(memory_space=pltpu.VMEM)
HBM = pl.BlockSpec(memory_space=pltpu.HBM)


def params(mib):
    return pltpu.CompilerParams(vmem_limit_bytes=int(mib * MIB))


def fetch(source, target, sems, first, parts):
    rows = source.shape[0] // parts
    copies = [
        pltpu.make_async_copy(
            source.at[pl.ds(i * rows, rows)], target.at[pl.ds(i * rows, rows)], sems.at[first + i]
        )
        for i in range(parts)
    ]
    for copy in copies:
        copy.start()
    return copies


def parts_of(rows):
    return 4 if rows % 64 == 0 else 1


class Chips:
    def __init__(self, devices):
        self.devices = devices
        self.count = devices // 2
        assert devices == 2 * self.count and self.count & (self.count - 1) == 0
        assert self.count > 2
        far = list(range(self.count - 1, 1, -1))
        self.steps = list(zip(far[0::2], far[1::2]))

    def swap(self, x):
        return lax.ppermute(x, "sec", [(i, i ^ 1) for i in range(self.devices)])

    def near(self, x):
        return lax.ppermute(x, "sec", [(i, i ^ 2) for i in range(self.devices)])

    def far(self, x, step):
        distances = self.steps[step]
        pairs = [(i, i ^ (2 * distances[i % 2])) for i in range(self.devices)]
        return lax.ppermute(x, "sec", pairs)

    def gather(self, both, mine):
        count = len(self.steps)
        received = [self.far(both, j) for j in range(count)]
        near = self.near(mine)
        swapped = [self.swap(r) for r in received]
        return [both] + received + swapped + [near, self.swap(near)]


def chip_ids(me, steps):
    core, chip = me % 2, me // 2
    mine = [chip ^ jnp.where(core == 0, a, b) for a, b in steps]
    others = [chip ^ jnp.where(core == 0, b, a) for a, b in steps]
    return [chip] + mine + others + [chip ^ 1]


def attention_kernel(
    me_ref, lens_ref, q_hbm, nk_hbm, nv_hbm, k_hbm, v_hbm, o_ref, q_ref, nk_ref, nv_ref, k_ref, v_ref, sems
):
    slots, positions = k_ref.shape[1], k_ref.shape[2]
    small = [
        pltpu.make_async_copy(a, b, sems.at[2 * KVH + i])
        for i, (a, b) in enumerate([(q_hbm, q_ref), (nk_hbm, nk_ref), (nv_hbm, nv_ref)])
    ]
    for copy in small:
        copy.start()
    large = []
    for k in range(KVH):
        for i, (a, b) in enumerate([(k_hbm, k_ref), (v_hbm, v_ref)]):
            copy = pltpu.make_async_copy(
                a.at[:, :, pl.ds(k * HD, HD)], b.at[k], sems.at[2 * k + i]
            )
            copy.start()
            large.append(copy)
    grouped = H // KVH
    rows = grouped * slots
    scaling = 1.0 / math.sqrt(HD)
    row_slot = lax.broadcasted_iota(jnp.int32, (rows, positions), 0) % slots
    position = lax.broadcasted_iota(jnp.int32, (rows, positions), 1)
    bias = jnp.concatenate(
        [
            jnp.where((row_slot == s) & (position < lens_ref[s]), 0.0, -jnp.inf)
            for s in range(slots)
        ],
        axis=1,
    )
    for copy in small:
        copy.wait()
    for k in range(KVH):
        at = slice(k * HD, (k + 1) * HD)
        heads = [slice((k * grouped + g) * HD, (k * grouped + g + 1) * HD) for g in range(grouped)]
        query = jnp.concatenate([q_ref[:, h].astype(F32) for h in heads], axis=0)
        large[2 * k].wait()
        keys = k_ref[k].reshape(slots * positions, HD)
        scores = lax.dot_general(query.astype(BF16), keys, NT, preferred_element_type=F32)
        scores = scores * scaling + bias
        new_key = jnp.concatenate([nk_ref[:, at].astype(F32)] * grouped, axis=0)
        fresh = jnp.sum(query * new_key, axis=1, keepdims=True) * scaling
        highest = jnp.maximum(jnp.max(scores, axis=1, keepdims=True), fresh)
        weights = jnp.exp(scores - highest)
        fresh_weight = jnp.exp(fresh - highest)
        inverse = 1.0 / (jnp.sum(weights, axis=1, keepdims=True) + fresh_weight)
        probs = (weights * inverse).astype(BF16)
        fresh_prob = (fresh_weight * inverse).astype(BF16).astype(F32)
        large[2 * k + 1].wait()
        values = v_ref[k].reshape(slots * positions, HD)
        mixture = jnp.dot(probs, values, preferred_element_type=F32)
        new_value = jnp.concatenate([nv_ref[:, at].astype(F32)] * grouped, axis=0)
        mixture = mixture + fresh_prob * new_value
        for g, h in enumerate(heads):
            o_ref[:, h] = mixture[g * slots : (g + 1) * slots].astype(BF16)


def attend(me, queries, new_keys, new_values, cache_keys, cache_values, cache_lengths):
    cache = pltpu.VMEM((KVH,) + cache_keys.shape[:2] + (HD,), BF16)
    return pl.pallas_call(
        attention_kernel,
        in_specs=[SMEM, SMEM] + [HBM] * 5,
        out_specs=VMEM,
        out_shape=jax.ShapeDtypeStruct(queries.shape, BF16),
        scratch_shapes=[
            pltpu.VMEM(queries.shape, BF16),
            pltpu.VMEM(new_keys.shape, BF16),
            pltpu.VMEM(new_values.shape, BF16),
            cache,
            cache,
            pltpu.SemaphoreType.DMA((2 * KVH + 3,)),
        ],
        compiler_params=params(56.5),
        name="attention",
    )(me, cache_lengths, queries, new_keys, new_values, cache_keys, cache_values)


def first_fetch_kernel(weight_hbm, residual_hbm, gain_ref, weight_ref, residual_ref, o_ref, sems):
    parts = parts_of(weight_hbm.shape[0])
    copies = fetch(weight_hbm, weight_ref, sems, 0, parts)
    copies += fetch(residual_hbm, residual_ref, sems, parts, 1)
    rows = o_ref.shape[1]

    @pl.loop(0, o_ref.shape[0], step=128)
    def _(c):
        at = pl.ds(pl.multiple_of(c, 128), 128)
        o_ref[at, :] = jnp.broadcast_to(gain_ref[:, at], (rows, 128)).T

    for copy in copies:
        copy.wait()


def first_fetch(out_weight, residual, norm_gain):
    width = norm_gain.shape[0]
    return pl.pallas_call(
        first_fetch_kernel,
        in_specs=[HBM, HBM, VMEM],
        out_specs=[VMEM] * 3,
        out_shape=[
            jax.ShapeDtypeStruct(out_weight.shape, BF16),
            jax.ShapeDtypeStruct(residual.shape, BF16),
            jax.ShapeDtypeStruct((width, residual.shape[1]), F32),
        ],
        scratch_shapes=[pltpu.SemaphoreType.DMA((parts_of(out_weight.shape[0]) + 1,))],
        compiler_params=params(40),
        name="fetch1",
    )(out_weight, residual, norm_gain.reshape(1, width))


def second_fetch_kernel(source, *refs):
    targets, sems = refs[:-1], refs[-1]
    rows = targets[0].shape[0]
    copies = [
        pltpu.make_async_copy(source.at[pl.ds(i * rows, rows)], target, sems.at[i])
        for i, target in enumerate(targets)
    ]
    for copy in copies:
        copy.start()
    for copy in copies:
        copy.wait()


def second_fetch(weight, tile, parts):
    return pl.pallas_call(
        second_fetch_kernel,
        in_specs=[HBM],
        out_specs=[VMEM] * parts,
        out_shape=[jax.ShapeDtypeStruct((tile, weight.shape[1]), BF16)] * parts,
        scratch_shapes=[pltpu.SemaphoreType.DMA((parts,))],
        compiler_params=params(42),
        name="fetch2",
    )(weight)


def pair_kernel(me_ref, mine_ref, other_ref, o_ref):
    place_halves(me_ref[0] % 2 == 0, mine_ref[...], other_ref[...], o_ref)


def place_halves(first, mine, other, o_ref):
    m = mine.shape[0]
    o_ref[:m, :] = jnp.where(first, mine, other)
    o_ref[m:, :] = jnp.where(first, other, mine)


def pair(me, mine, other):
    m, rows = mine.shape
    return pl.pallas_call(
        pair_kernel,
        in_specs=[SMEM, VMEM, VMEM],
        out_specs=VMEM,
        out_shape=jax.ShapeDtypeStruct((2 * m, rows), BF16),
        compiler_params=params(4),
        name="pair",
    )(me, mine, other)


def projection_kernel(steps, me_ref, rows_ref, weight_ref, residual_ref, *refs):
    pieces = 2 * len(steps) + 3
    piece_refs, o_ref, slots_ref = refs[:pieces], refs[pieces], refs[pieces + 1]
    local = piece_refs[-1].shape[0]
    for i, ref in enumerate(piece_refs[:-2]):
        slots_ref[2 * local * i : 2 * local * (i + 1), :] = ref[...]
    near = jnp.concatenate([ref[...].astype(F32) for ref in piece_refs[-2:]])
    slots_ref[2 * local * (pieces - 2) :, :] = near.astype(BF16)

    me = me_ref[0]
    chips = chip_ids(me, steps)
    slots, rows = slots_ref.shape[0], rows_ref.shape[1]
    at = lax.broadcasted_iota(jnp.int32, (slots, rows), 0)
    held = at % local
    for i, chip in enumerate(chips):
        core = (me + (1 if len(steps) < i <= 2 * len(steps) else 0)) % 2
        for j, device in enumerate([2 * chip + core, 2 * chip + 1 - core]):
            held += jnp.where(at // local == 2 * i + j, device * local, 0)
    pick = jnp.where(held == rows_ref[...], 1.0, 0.0).T.astype(BF16)

    width = weight_ref.shape[1]
    part = min(width, 1024)
    total = residual_ref[...].astype(F32)
    for c in range(0, width, part):
        ordered = jnp.dot(pick, slots_ref[:, c : c + part], preferred_element_type=F32)
        total += lax.dot_general(
            weight_ref[:, c : c + part], ordered.astype(BF16), NT, preferred_element_type=F32
        )
    o_ref[...] = total.astype(BF16)


def project(steps, me, slot_of_row, out_weight, residual, pieces):
    m, rows = residual.shape
    return pl.pallas_call(
        functools.partial(projection_kernel, steps),
        in_specs=[SMEM] + [VMEM] * (3 + len(pieces)),
        out_specs=VMEM,
        out_shape=jax.ShapeDtypeStruct((m, rows), BF16),
        scratch_shapes=[pltpu.VMEM((rows, out_weight.shape[1]), BF16)],
        compiler_params=params(12),
        name="projection",
    )(me, slot_of_row.reshape(1, rows), out_weight, residual, *pieces)


def hidden_kernel(steps, tile, me_ref, gain_ref, gate_hbm, up_hbm, down_hbm, *refs):
    pieces = 2 * len(steps) + 3
    piece_refs, up_refs = refs[:pieces], refs[pieces:-7]
    o_ref, down_ref, gate_ref, rest_ref, x_ref, near_ref, sems = refs[-7:]
    parts = gate_hbm.shape[0] // tile
    held = len(up_refs)
    gate_copies, up_copies = [], []
    for i in range(parts):
        rows = pl.ds(i * tile, tile)
        copy = pltpu.make_async_copy(gate_hbm.at[rows], gate_ref.at[rows], sems.at[i])
        copy.start()
        gate_copies.append(copy)
        if i >= held:
            copy = pltpu.make_async_copy(
                up_hbm.at[rows], rest_ref.at[pl.ds((i - held) * tile, tile)], sems.at[parts + i]
            )
            copy.start()
            up_copies.append(copy)
    copies = fetch(down_hbm, down_ref, sems, 2 * parts, parts_of(down_hbm.shape[0]))
    wide = piece_refs[0].shape[0]
    me = me_ref[0]
    place_halves(me % 2 == 0, piece_refs[-2][...], piece_refs[-1][...], near_ref)
    squares = None
    for chip, ref in zip(chip_ids(me, steps), list(piece_refs[:-2]) + [near_ref]):
        at = pl.ds(pl.multiple_of(chip * wide, 128), wide)
        value = ref[...].astype(F32)
        x_ref[at, :] = (value * gain_ref[at, :]).astype(BF16)
        square = value * value
        squares = square if squares is None else squares + square
    mean = jnp.sum(squares, axis=0, keepdims=True) * (1.0 / x_ref.shape[0])
    scale = lax.rsqrt(mean + EPSILON)
    for i in range(parts):
        at = slice(i * tile, (i + 1) * tile)
        if i < held:
            weights = up_refs[i][...]
        else:
            up_copies[i - held].wait()
            weights = rest_ref[(i - held) * tile : (i - held + 1) * tile, :]
        up = jnp.dot(weights, x_ref[...], preferred_element_type=F32) * scale
        gate_copies[i].wait()
        gate = jnp.dot(gate_ref[at, :], x_ref[...], preferred_element_type=F32) * scale
        units = gate / (1.0 + jnp.exp(-gate)) * up
        o_ref[:, at] = units.T.astype(BF16)
    for copy in copies:
        copy.wait()


def unit_tile(units):
    return 256 if units % 256 == 0 else units


def hidden_units(steps, me, gain, gate_weight, up_weight, up_held, down_weight, pieces):
    units, width = gate_weight.shape
    wide, rows = pieces[0].shape
    tile = unit_tile(units)
    return pl.pallas_call(
        functools.partial(hidden_kernel, steps, tile),
        in_specs=[SMEM, VMEM, HBM, HBM, HBM] + [VMEM] * (len(pieces) + len(up_held)),
        out_specs=[VMEM, VMEM],
        out_shape=[
            jax.ShapeDtypeStruct((rows, units), BF16),
            jax.ShapeDtypeStruct(down_weight.shape, BF16),
        ],
        scratch_shapes=[
            pltpu.VMEM(gate_weight.shape, BF16),
            pltpu.VMEM((max(units - len(up_held) * tile, 16), width), BF16),
            pltpu.VMEM((width, rows), BF16),
            pltpu.VMEM((wide, rows), BF16),
            pltpu.SemaphoreType.DMA((2 * (units // tile) + parts_of(units),)),
        ],
        compiler_params=params(25),
        name="hidden",
    )(me, gain, gate_weight, up_weight, down_weight, *pieces, *up_held)


def down_block(hidden_ref, weight_ref, chip, wide):
    at = pl.ds(pl.multiple_of(chip * wide, 128), wide)
    return jnp.dot(hidden_ref[...], weight_ref[:, at], preferred_element_type=F32)


def theirs_kernel(steps, me_ref, hidden_ref, weight_ref, o_ref):
    chips = chip_ids(me_ref[0], steps)
    count = len(steps)
    for j, chip in enumerate(chips[count + 1 :] + chips[:1]):
        o_ref[j] = down_block(hidden_ref, weight_ref, chip, o_ref.shape[2]).astype(BF16)


def partial_sums(steps, me, hidden, down_weight, wide):
    return pl.pallas_call(
        functools.partial(theirs_kernel, steps),
        in_specs=[SMEM, VMEM, VMEM],
        out_specs=VMEM,
        out_shape=jax.ShapeDtypeStruct((len(steps) + 2, hidden.shape[0], wide), BF16),
        compiler_params=params(12),
        name="theirs",
    )(me, hidden, down_weight)


def mine_kernel(steps, me_ref, hidden_ref, weight_ref, own_ref, swapped_ref, *o_refs):
    me = me_ref[0]
    chips = chip_ids(me, steps)
    count = len(steps)
    for j in range(count):
        total = down_block(hidden_ref, weight_ref, chips[1 + j], o_refs[j].shape[1])
        o_refs[j][...] = (total + swapped_ref[j].astype(F32)).astype(BF16)
    near = own_ref[count].astype(F32) + swapped_ref[count].astype(F32)
    o_refs[count][...] = half_of(me % 2, near).astype(BF16)


def chip_sums(steps, me, hidden, down_weight, own, swapped):
    rows, wide = own.shape[1:]
    return pl.pallas_call(
        functools.partial(mine_kernel, steps),
        in_specs=[SMEM] + [VMEM] * 4,
        out_specs=[VMEM] * (len(steps) + 1),
        out_shape=[jax.ShapeDtypeStruct((rows, wide), BF16)] * len(steps)
        + [jax.ShapeDtypeStruct((rows, wide // 2), BF16)],
        compiler_params=params(12),
        name="mine",
    )(me, hidden, down_weight, own, swapped)


def half_of(core, value):
    m = value.shape[1] // 2
    return jnp.where(core == 0, value[:, :m], value[:, m:])


def received_sum(refs):
    total = refs[0][...].astype(F32)
    for ref in refs[1:]:
        total += ref[...].astype(F32)
    return total


def handover_kernel(me_ref, *refs):
    refs[-1][...] = half_of(1 - me_ref[0] % 2, received_sum(refs[:-1])).astype(BF16)


def handover(me, received):
    rows, wide = received[0].shape
    return pl.pallas_call(
        handover_kernel,
        in_specs=[SMEM] + [VMEM] * len(received),
        out_specs=VMEM,
        out_shape=jax.ShapeDtypeStruct((rows, wide // 2), BF16),
        compiler_params=params(12),
        name="handover",
    )(me, *received)


def output_kernel(me_ref, stream_ref, own_ref, owns_ref, near_ref, hand_ref, *refs):
    last = own_ref.shape[0] - 1
    total = received_sum(refs[:-1])
    total += own_ref[last].astype(F32) + owns_ref[last].astype(F32)
    total = half_of(me_ref[0] % 2, total) + near_ref[...].astype(F32) + hand_ref[...].astype(F32)
    refs[-1][...] = (stream_ref[...].astype(F32) + total.T).astype(BF16)


def output(me, stream, own, swapped, near, hand, received):
    m, rows = stream.shape
    return pl.pallas_call(
        output_kernel,
        in_specs=[SMEM] + [VMEM] * (5 + len(received)),
        out_specs=VMEM,
        out_shape=jax.ShapeDtypeStruct((m, rows), BF16),
        compiler_params=params(12),
        name="output",
    )(me, stream, own, swapped, near, hand, *received)


def on_device(
    residual,
    queries,
    new_keys,
    new_values,
    cache_keys,
    cache_values,
    cache_lengths,
    slot_of_row,
    out_weight,
    norm_gain,
    gate_weight,
    up_weight,
    down_weight,
):
    chips = Chips(lax.axis_size("sec"))
    steps = chips.steps
    me = lax.axis_index("sec").reshape(1)
    wide = 2 * residual.shape[0]

    attended = attend(me, queries, new_keys, new_values, cache_keys, cache_values, cache_lengths)
    both = jnp.concatenate([attended, chips.swap(attended)])
    out_weight, residual, gain = first_fetch(out_weight, residual, norm_gain)
    pieces = chips.gather(both, attended)
    stream = project(steps, me, slot_of_row, out_weight, residual, pieces)

    other = chips.swap(stream)
    both = pair(me, stream, other)
    tile = unit_tile(up_weight.shape[0])
    up_held = second_fetch(up_weight, tile, (up_weight.shape[0] // tile + 1) // 2)
    pieces = chips.gather(both, stream)
    hidden, down_weight = hidden_units(
        steps, me, gain, gate_weight, up_weight, up_held, down_weight, pieces
    )

    own = partial_sums(steps, me, hidden, down_weight, wide)
    own_swapped = chips.swap(own)
    *sums, near_sum = chip_sums(steps, me, hidden, down_weight, own, own_swapped)
    received = [chips.far(x, j) for j, x in enumerate(sums)]
    near = chips.near(near_sum)
    hand = chips.swap(handover(me, received))
    return output(me, stream, own, own_swapped, near, hand, received)


def solution(mesh):
    in_specs = (
        P("sec", "group"),
        P(("group", "sec"), None),
        P(("group", "sec"), None),
        P(("group", "sec"), None),
        P(("group", "sec"), None, None),
        P(("group", "sec"), None, None),
        P(("group", "sec")),
        P("group"),
        P("sec", None),
        P(),
        P("sec", None),
        P("sec", None),
        P("sec", None),
    )
    out_specs = P("sec", "group")

    return jax.shard_map(
        on_device, mesh=mesh, in_specs=in_specs, out_specs=out_specs, check_vma=False
    )
```

time: 192 us -> 86.7 us (0.45)
  waiting for transfers between devices: 129 us -> 31.9 us
  matrix products: 33.9 us -> 0 us
  Pallas kernels: 0 us -> 29.1 us
  starting transfers between devices: 0.09 us -> 24.5 us
  between operations: 13.3 us -> 0.17 us
  other arithmetic: 9.64 us -> 0.85 us
  local copies, waits for them, and re-layouts: 5.86 us -> 0.01 us
    all_gather x2 -> x0, waiting for transfers between devices: 71.4 us -> none  [the longest x1 35.7 us: on_device(): gathered = lax.all_gather(stream, 'sec', axis=0, tiled=True)]
    reduce_scatter x1 -> x0, waiting for transfers between devices: 57.6 us -> none  [on_device(): lax.psum_scatter(lax.dot_general(down_weight, hidden, (((0,), (0,)), ((),...]
    dot_general x6 -> x0, matrix products: 33.9 us -> none  [the longest x1 15.1 us: on_device(): lax.dot_general(down_weight, hidden, (((0,), (0,)), ((), ())), preferred_...]
    ppermute x0 -> x24, waiting for transfers between devices: none -> 31.9 us  [the longest x9 26.9 us: far(): return lax.ppermute(x, 'sec', pairs)]
    pallas_call x0 -> x10, Pallas kernels: none -> 29.1 us  [the longest x1 12.4 us: hidden_units(): pl.pallas_call(functools.partial(hidden_kernel, steps, tile), in_specs=[S...]
    ppermute x0 -> x24, starting transfers between devices: none -> 24.5 us  [the longest x9 19.1 us: far(): return lax.ppermute(x, 'sec', pairs)]
    sort x2 -> x0, other arithmetic: 5.21 us -> none  [the longest x1 2.61 us: on_device(): inverse = jnp.argsort(slot_of_row)]
    gather x4 -> x0, local copies, waits for them, and re-layouts: 4.15 us -> none  [the longest x2 2.07 us: on_device(): return jnp.take(outputs, position_of[slot_of_row], axis=1)]
  transfers between devices with their start and end apart: 3 -> 24, of which waited for: 3 -> 10; matrix products, arithmetic and copies ran while one was open for 5% -> 0% of each run, Pallas kernels for 0% -> 8%
where the time goes in v1:
time: 86.7 us; the launch traced here: 86.5 us
  waiting for transfers between devices  31.9 us (37%)
  Pallas kernels  29.1 us (34%)
  starting transfers between devices  24.5 us (28%)
    ppermute x9, waiting for transfers between devices, far(): return lax.ppermute(x, 'sec', pairs)  26.9 us
    ppermute x9, starting transfers between devices, far(): return lax.ppermute(x, 'sec', pairs)  19.1 us
    pallas_call x1, Pallas kernels, hidden_units(): pl.pallas_call(functools.partial(hidden_kernel, steps, tile), in_specs=[S...  12.4 us
    ppermute x12, waiting for transfers between devices, swap(): return lax.ppermute(x, 'sec', [(i, i ^ 1) for i in range(self.devices)])  4.99 us
    pallas_call x1, Pallas kernels, attend(): pl.pallas_call(attention_kernel, in_specs=[SMEM, SMEM] + [HBM] * 5, out_s...  4.88 us
    pallas_call x1, Pallas kernels, second_fetch(): pl.pallas_call(second_fetch_kernel, in_specs=[HBM], out_specs=[VMEM] * pa...  3.5 us
    pallas_call x1, Pallas kernels, first_fetch(): pl.pallas_call(first_fetch_kernel, in_specs=[HBM, HBM, VMEM], out_specs=[...  3.48 us
    ppermute x12, starting transfers between devices, swap(): return lax.ppermute(x, 'sec', [(i, i ^ 1) for i in range(self.devices)])  2.9 us
  transfers between devices with their start and end apart: 24, of which 10 were waited for; matrix products, arithmetic and copies ran while one was open for 0% of the time, Pallas kernels for 8%

profile of v1, /device:TPU:0, one launch (start us, length us, event | category | flops | bytes accessed | tf_op | source)
XLA Modules:
  0.0 86.5 jit_solution(10165174124018551124)
XLA Ops:
  0.0 0.0 copy-start.2
  0.0 0.0 copy-start
  0.0 4.9 %attention.1 = bf16[8,4096]{1,0:T(8,128)(2,1)} custom-call(s32[1]{0:T(128)} %bitcast.me_ref, s32[8]{0:T(128)} %lens_ref.1, bf16[8,4096]{1,0:T(8,128)(2,1)} %q_hbm.1, bf16[8,512]{1,0:T(8,128)(2,1)} %nk_hbm.1, bf16[8,512]{1,0:T(8,128)(2,1)} %nv_hbm.1, bf16[8,128,512]{2,1,0:T(8,128)(2,1)} %k_hbm.1, bf16[8,128,512]{2,1,0:T(8,128)(2,1)} %v_hbm.1), custom_call_target="tpu_custom_call" | custom-call | tf_op jit(solution)/shard_map/attention/pallas_call | solution.py:144
  4.9 0.6 collective-permute-start
  5.5 1.1 %collective-permute-done = bf16[8,4096]{1,0:T(8,128)(2,1)S(1)} collective-permute-done((bf16[8,4096]{1,0:T(8,128)(2,1)}, bf16[8,4096]{1,0:T(8,128)(2,1)S(1)}, u32[]{:S(2)}, u32[]{:S(2)}) %collective-permute-start) | collective-permute-done | bytes 65568 | tf_op jit(solution)/shard_map/ppermute | solution.py:60
  6.6 0.8 pad_maximum_fusion.refs_0_
  7.4 3.9 %collective-permute-start.3 = (bf16[16,4096]{1,0:T(8,128)(2,1)S(1)}, bf16[16,4096]{1,0:T(8,128)(2,1)S(1)}, u32[]{:S(2)}, u32[]{:S(2)}) collective-permute-start(bf16[16,4096]{1,0:T(8,128)(2,1)S(1)} %pad_maximum_fusion.refs_0_), channel_id=1, source_target_pairs={{0,6},{1,5},{2,4},{3,7},{4,2},{5,1},{6,0},{7,3},{8,14},{9,13},{10,... | collective-permute-start | bytes 393224 | tf_op jit(solution)/shard_map/ppermute | solution.py:68
  11.4 2.5 %collective-permute-start.2 = (bf16[16,4096]{1,0:T(8,128)(2,1)S(1)}, bf16[16,4096]{1,0:T(8,128)(2,1)S(1)}, u32[]{:S(2)}, u32[]{:S(2)}) collective-permute-start(bf16[16,4096]{1,0:T(8,128)(2,1)S(1)} %pad_maximum_fusion.refs_0_), channel_id=1, source_target_pairs={{0,10},{1,9},{2,8},{3,11},{4,14},{5,13},{6,12},{7,15},{8,2},{9,1},... | collective-permute-start | bytes 393224 | tf_op jit(solution)/shard_map/ppermute | solution.py:68
  13.9 1.2 %collective-permute-start.1 = (bf16[16,4096]{1,0:T(8,128)(2,1)S(1)}, bf16[16,4096]{1,0:T(8,128)(2,1)S(1)}, u32[]{:S(2)}, u32[]{:S(2)}) collective-permute-start(bf16[16,4096]{1,0:T(8,128)(2,1)S(1)} %pad_maximum_fusion.refs_0_), channel_id=1, source_target_pairs={{0,14},{1,13},{2,12},{3,15},{4,10},{5,9},{6,8},{7,11},{8,6},{9,5},... | collective-permute-start | bytes 393224 | tf_op jit(solution)/shard_map/ppermute | solution.py:68
  15.1 0.3 collective-permute-start.7
  15.4 1.3 %collective-permute-done.3.refs_3_ = bf16[16,4096]{1,0:T(8,128)(2,1)S(1)} collective-permute-done((bf16[16,4096]{1,0:T(8,128)(2,1)S(1)}, bf16[16,4096]{1,0:T(8,128)(2,1)S(1)}, u32[]{:S(2)}, u32[]{:S(2)}) %collective-permute-start.3) | collective-permute-done | bytes 131104 | tf_op jit(solution)/shard_map/ppermute | solution.py:68
  16.8 0.0 collective-permute-start.6
  16.8 7.8 %collective-permute-done.2.refs_2_ = bf16[16,4096]{1,0:T(8,128)(2,1)S(1)} collective-permute-done((bf16[16,4096]{1,0:T(8,128)(2,1)S(1)}, bf16[16,4096]{1,0:T(8,128)(2,1)S(1)}, u32[]{:S(2)}, u32[]{:S(2)}) %collective-permute-start.2) | collective-permute-done | bytes 131104 | tf_op jit(solution)/shard_map/ppermute | solution.py:68
  24.6 0.0 collective-permute-start.5
  24.6 0.0 collective-permute-done.1.refs_1_
  24.6 0.5 collective-permute-start.4
  25.1 0.0 collective-permute-done.7.refs_7_
  25.1 0.1 collective-permute-start.8
  25.2 0.0 copy-done.2
  25.2 0.0 copy-done
  25.2 0.0 copy-done.1
  25.2 3.5 %fetch1.1 = (bf16[256,4096]{1,0:T(8,128)(2,1)S(1)}, bf16[256,128]{1,0:T(8,128)(2,1)S(1)}, f32[4096,128]{1,0:T(8,128)S(1)}) custom-call(bf16[256,4096]{1,0:T(8,128)(2,1)S(1)} %copy-done, bf16[256,128]{1,0:T(8,128)(2,1)S(1)} %copy-done.1, f32[1,4096]{1,0:T(1,128)S(1)} %bitcast.3), custom_call_target="tpu_custom_call" | custom-call | tf_op jit(solution)/shard_map/fetch1/pallas_call | solution.py:179
  28.7 0.0 collective-permute-done.8.refs_8_
  28.7 0.0 collective-permute-done.6.refs_6_
  28.7 0.0 collective-permute-done.5.refs_5_
  28.7 0.0 collective-permute-done.4.refs_4_
  28.7 0.0 copy-done.3
  28.8 1.6 %projection.1.mine_ref.stream_ref = bf16[256,128]{1,0:T(8,128)(2,1)S(1)} custom-call(s32[1]{0:T(128)} %bitcast.me_ref, s32[1,128]{1,0:T(1,128)S(1)} %bitcast.4, bf16[256,4096]{1,0:T(8,128)(2,1)S(1)} %get-tuple-element.18.weight_ref, bf16[256,128]{1,0:T(8,128)(2,1)S(1)} %get-tuple-element.19.residual_ref, bf16[16,4096]{1,0:T(8,128)(2,1)S(1)} %pad_maximum_fusion.refs_0_, ...), custom_call_target="tpu_custom_call" | custom-call | tf_op jit(solution)/shard_map/projection/pallas_call | solution.py:274
  30.4 0.5 collective-permute-start.9
  30.9 0.9 %collective-permute-done.9.other_ref = bf16[256,128]{1,0:T(8,128)(2,1)S(1)} collective-permute-done((bf16[256,128]{1,0:T(8,128)(2,1)S(1)}, bf16[256,128]{1,0:T(8,128)(2,1)S(1)}, u32[]{:S(2)}, u32[]{:S(2)}) %collective-permute-start.9) | collective-permute-done | bytes 65568 | tf_op jit(solution)/shard_map/ppermute | solution.py:60
  31.8 1.8 %collective-permute-start.12 = (bf16[512,128]{1,0:T(8,128)(2,1)S(1)}, bf16[512,128]{1,0:T(8,128)(2,1)S(1)}, u32[]{:S(2)}, u32[]{:S(2)}) collective-permute-start(bf16[512,128]{1,0:T(8,128)(2,1)S(1)} %pair.1.refs_0_), channel_id=1, source_target_pairs={{0,6},{1,5},{2,4},{3,7},{4,2},{5,1},{6,0},{7,3},{8,14},{9,13},{10,... | collective-permute-start | bytes 393224 | tf_op jit(solution)/shard_map/ppermute | solution.py:68
  33.6 2.2 %collective-permute-start.11 = (bf16[512,128]{1,0:T(8,128)(2,1)S(1)}, bf16[512,128]{1,0:T(8,128)(2,1)S(1)}, u32[]{:S(2)}, u32[]{:S(2)}) collective-permute-start(bf16[512,128]{1,0:T(8,128)(2,1)S(1)} %pair.1.refs_0_), channel_id=1, source_target_pairs={{0,10},{1,9},{2,8},{3,11},{4,14},{5,13},{6,12},{7,15},{8,2},{9,1},... | collective-permute-start | bytes 393224 | tf_op jit(solution)/shard_map/ppermute | solution.py:68
  35.8 1.3 %collective-permute-start.10 = (bf16[512,128]{1,0:T(8,128)(2,1)S(1)}, bf16[512,128]{1,0:T(8,128)(2,1)S(1)}, u32[]{:S(2)}, u32[]{:S(2)}) collective-permute-start(bf16[512,128]{1,0:T(8,128)(2,1)S(1)} %pair.1.refs_0_), channel_id=1, source_target_pairs={{0,14},{1,13},{2,12},{3,15},{4,10},{5,9},{6,8},{7,11},{8,6},{9,5},... | collective-permute-start | bytes 393224 | tf_op jit(solution)/shard_map/ppermute | solution.py:68
  37.1 1.5 %collective-permute-start.16 = (bf16[256,128]{1,0:T(8,128)(2,1)S(1)}, bf16[256,128]{1,0:T(8,128)(2,1)S(1)}, u32[]{:S(2)}, u32[]{:S(2)}) collective-permute-start(bf16[256,128]{1,0:T(8,128)(2,1)S(1)} %projection.1.mine_ref.stream_ref), channel_id=1, source_target_pairs={{0,2},{1,3},{2,0},{3,1},{4,6},{5,7},{6,4},{7,5},{8,10},{9,11},{10,... | collective-permute-start | bytes 196616 | tf_op jit(solution)/shard_map/ppermute | solution.py:63
  38.6 0.6 collective-permute-done.12.refs_3_
  39.2 0.0 collective-permute-start.15
  39.2 7.6 %collective-permute-done.11.refs_2_ = bf16[512,128]{1,0:T(8,128)(2,1)S(1)} collective-permute-done((bf16[512,128]{1,0:T(8,128)(2,1)S(1)}, bf16[512,128]{1,0:T(8,128)(2,1)S(1)}, u32[]{:S(2)}, u32[]{:S(2)}) %collective-permute-start.11) | collective-permute-done | bytes 131104 | tf_op jit(solution)/shard_map/ppermute | solution.py:68
  46.8 0.0 collective-permute-start.14
  46.8 0.0 collective-permute-done.10.refs_1_
  46.8 0.5 collective-permute-start.13
  47.3 0.0 collective-permute-done.16.refs_7_
  47.3 0.1 collective-permute-start.17
  47.4 3.5 %fetch2.1 = (bf16[256,4096]{1,0:T(8,128)(2,1)S(1)}, bf16[256,4096]{1,0:T(8,128)(2,1)S(1)}, bf16[256,4096]{1,0:T(8,128)(2,1)S(1)}, bf16[256,4096]{1,0:T(8,128)(2,1)S(1)}) custom-call(bf16[1792,4096]{1,0:T(8,128)(2,1)} %up_hbm.1), custom_call_target="tpu_custom_call" | custom-call | tf_op jit(solution)/shard_map/fetch2/pallas_call | solution.py:208
  50.9 0.0 collective-permute-done.17.refs_8_
  50.9 0.0 collective-permute-done.15.refs_6_
  50.9 0.0 collective-permute-done.14.refs_5_
  51.0 0.0 collective-permute-done.13.refs_4_
  51.0 12.4 %hidden.1 = (bf16[128,1792]{1,0:T(8,128)(2,1)S(1)}, bf16[1792,4096]{1,0:T(8,128)(2,1)S(1)}) custom-call(s32[1]{0:T(128)} %bitcast.me_ref, f32[4096,128]{1,0:T(8,128)S(1)} %get-tuple-element.20.gain_ref, bf16[1792,4096]{1,0:T(8,128)(2,1)} %gate_hbm.1, bf16[1792,4096]{1,0:T(8,128)(2,1)} %up_hbm.1, bf16[1792,4096]{1,0:T(8,128)(2,1)} %down_hbm.1, ...), custom_call_target="tpu_custom_call" | custom-call | tf_op jit(solution)/shard_map/hidden/pallas_call | solution.py:340
  63.4 1.4 %theirs.1.own_ref = bf16[5,128,512]{2,1,0:T(8,128)(2,1)S(1)} custom-call(s32[1]{0:T(128)} %bitcast.me_ref, bf16[128,1792]{1,0:T(8,128)(2,1)S(1)} %get-tuple-element.25.hidden_ref, bf16[1792,4096]{1,0:T(8,128)(2,1)S(1)} %get-tuple-element.26.weight_ref), custom_call_target="tpu_custom_call" | custom-call | tf_op jit(solution)/shard_map/theirs/pallas_call | solution.py:373
  64.8 0.6 collective-permute-start.18
  65.3 1.7 %collective-permute-done.18.swapped_ref.owns_ref = bf16[5,128,512]{2,1,0:T(8,128)(2,1)S(1)} collective-permute-done((bf16[5,128,512]{2,1,0:T(8,128)(2,1)S(1)}, bf16[5,128,512]{2,1,0:T(8,128)(2,1)S(1)}, u32[]{:S(2)}, u32[]{:S(2)}) %collective-permute-start.18) | collective-permute-done | bytes 655392 | tf_op jit(solution)/shard_map/ppermute | solution.py:60
  67.1 1.0 %mine.1 = (bf16[128,512]{1,0:T(8,128)(2,1)S(1)}, bf16[128,512]{1,0:T(8,128)(2,1)S(1)}, bf16[128,512]{1,0:T(8,128)(2,1)S(1)}, bf16[128,256]{1,0:T(8,128)(2,1)S(1)}) custom-call(s32[1]{0:T(128)} %bitcast.me_ref, bf16[128,1792]{1,0:T(8,128)(2,1)S(1)} %get-tuple-element.25.hidden_ref, bf16[1792,4096]{1,0:T(8,128)(2,1)S(1)} %get-tuple-element.26.weight_ref, ...), custom_call_target="tpu_custom_call" | custom-call | tf_op jit(solution)/shard_map/mine/pallas_call | solution.py:396
  68.1 3.3 %collective-permute-start.20 = (bf16[128,512]{1,0:T(8,128)(2,1)S(1)}, bf16[128,512]{1,0:T(8,128)(2,1)S(1)}, u32[]{:S(2)}, u32[]{:S(2)}) collective-permute-start(bf16[128,512]{1,0:T(8,128)(2,1)S(1)} %get-tuple-element.28), channel_id=1, source_target_pairs={{0,14},{1,13},{2,12},{3,15},{4,10},{5,9},{6,8},{7,11},{8,6},{9,5},... | collective-permute-start | bytes 393224 | tf_op jit(solution)/shard_map/ppermute | solution.py:68
  71.4 0.9 %collective-permute-start.21 = (bf16[128,512]{1,0:T(8,128)(2,1)S(1)}, bf16[128,512]{1,0:T(8,128)(2,1)S(1)}, u32[]{:S(2)}, u32[]{:S(2)}) collective-permute-start(bf16[128,512]{1,0:T(8,128)(2,1)S(1)} %get-tuple-element.29), channel_id=1, source_target_pairs={{0,10},{1,9},{2,8},{3,11},{4,14},{5,13},{6,12},{7,15},{8,2},{9,1},... | collective-permute-start | bytes 393224 | tf_op jit(solution)/shard_map/ppermute | solution.py:68
  72.3 2.0 %collective-permute-start.22 = (bf16[128,512]{1,0:T(8,128)(2,1)S(1)}, bf16[128,512]{1,0:T(8,128)(2,1)S(1)}, u32[]{:S(2)}, u32[]{:S(2)}) collective-permute-start(bf16[128,512]{1,0:T(8,128)(2,1)S(1)} %get-tuple-element.30), channel_id=1, source_target_pairs={{0,6},{1,5},{2,4},{3,7},{4,2},{5,1},{6,0},{7,3},{8,14},{9,13},{10,... | collective-permute-start | bytes 393224 | tf_op jit(solution)/shard_map/ppermute | solution.py:68
  74.3 0.6 collective-permute-start.19
  74.9 2.4 %collective-permute-done.20.refs_0_ = bf16[128,512]{1,0:T(8,128)(2,1)S(1)} collective-permute-done((bf16[128,512]{1,0:T(8,128)(2,1)S(1)}, bf16[128,512]{1,0:T(8,128)(2,1)S(1)}, u32[]{:S(2)}, u32[]{:S(2)}) %collective-permute-start.20) | collective-permute-done | bytes 131104 | tf_op jit(solution)/shard_map/ppermute | solution.py:68
  77.3 7.0 %collective-permute-done.21.refs_1_ = bf16[128,512]{1,0:T(8,128)(2,1)S(1)} collective-permute-done((bf16[128,512]{1,0:T(8,128)(2,1)S(1)}, bf16[128,512]{1,0:T(8,128)(2,1)S(1)}, u32[]{:S(2)}, u32[]{:S(2)}) %collective-permute-start.21) | collective-permute-done | bytes 131104 | tf_op jit(solution)/shard_map/ppermute | solution.py:68
  84.3 0.0 collective-permute-done.22.refs_2_
  84.4 0.1 handover.1
  84.4 0.1 collective-permute-start.23
  84.5 0.0 collective-permute-done.19.near_ref
  84.5 1.2 %collective-permute-done.23.hand_ref = bf16[128,256]{1,0:T(8,128)(2,1)S(1)} collective-permute-done((bf16[128,256]{1,0:T(8,128)(2,1)S(1)}, bf16[128,256]{1,0:T(8,128)(2,1)S(1)}, u32[]{:S(2)}, u32[]{:S(2)}) %collective-permute-start.23) | collective-permute-done | bytes 65568 | tf_op jit(solution)/shard_map/ppermute | solution.py:60
  85.7 0.8 output.1
  (3 shorter events, 0.0 us)
Async XLA Ops:
  0.0 25.2 %copy-start.2 = (f32[4096]{0:T(1024)S(1)}, f32[4096]{0:T(1024)}, u32[]{:S(2)}) copy-start(f32[4096]{0:T(1024)} %param.22) | copy-start | bytes 49156
  0.0 25.2 %copy-start = (bf16[256,4096]{1,0:T(8,128)(2,1)S(1)}, bf16[256,4096]{1,0:T(8,128)(2,1)}, u32[]{:S(2)}) copy-start(bf16[256,4096]{1,0:T(8,128)(2,1)} %weight_hbm.1) | copy-start | bytes 6291460
  0.0 25.2 %copy-start.1 = (bf16[256,128]{1,0:T(8,128)(2,1)S(1)}, bf16[256,128]{1,0:T(8,128)(2,1)}, u32[]{:S(2)}) copy-start(bf16[256,128]{1,0:T(8,128)(2,1)} %residual_hbm.1) | copy-start | bytes 196612
  0.0 28.7 %copy-start.3 = (s32[128]{0:T(128)S(1)}, s32[128]{0:T(128)}, u32[]{:S(2)}) copy-start(s32[128]{0:T(128)} %param.20) | copy-start | bytes 1540
  4.9 1.7 %collective-permute-start = (bf16[8,4096]{1,0:T(8,128)(2,1)}, bf16[8,4096]{1,0:T(8,128)(2,1)S(1)}, u32[]{:S(2)}, u32[]{:S(2)}) collective-permute-start(bf16[8,4096]{1,0:T(8,128)(2,1)} %attention.1), channel_id=1, source_target_pairs={{0,1},{1,0},{2,3},{3,2},{4,5},{5,4},{6,7},{7,6},{8,9},{9,8},{10,11... | collective-permute-start | bytes 196616 | tf_op jit(solution)/shard_map/ppermute | solution.py:60
  7.4 9.3 %collective-permute-start.3 = (bf16[16,4096]{1,0:T(8,128)(2,1)S(1)}, bf16[16,4096]{1,0:T(8,128)(2,1)S(1)}, u32[]{:S(2)}, u32[]{:S(2)}) collective-permute-start(bf16[16,4096]{1,0:T(8,128)(2,1)S(1)} %pad_maximum_fusion.refs_0_), channel_id=1, source_target_pairs={{0,6},{1,5},{2,4},{3,7},{4,2},{5,1},{6,0},{7,3},{8,14},{9,13},{10,... | collective-permute-start | bytes 393224 | tf_op jit(solution)/shard_map/ppermute | solution.py:68
  11.4 13.2 %collective-permute-start.2 = (bf16[16,4096]{1,0:T(8,128)(2,1)S(1)}, bf16[16,4096]{1,0:T(8,128)(2,1)S(1)}, u32[]{:S(2)}, u32[]{:S(2)}) collective-permute-start(bf16[16,4096]{1,0:T(8,128)(2,1)S(1)} %pad_maximum_fusion.refs_0_), channel_id=1, source_target_pairs={{0,10},{1,9},{2,8},{3,11},{4,14},{5,13},{6,12},{7,15},{8,2},{9,1},... | collective-permute-start | bytes 393224 | tf_op jit(solution)/shard_map/ppermute | solution.py:68
  13.9 10.7 %collective-permute-start.1 = (bf16[16,4096]{1,0:T(8,128)(2,1)S(1)}, bf16[16,4096]{1,0:T(8,128)(2,1)S(1)}, u32[]{:S(2)}, u32[]{:S(2)}) collective-permute-start(bf16[16,4096]{1,0:T(8,128)(2,1)S(1)} %pad_maximum_fusion.refs_0_), channel_id=1, source_target_pairs={{0,14},{1,13},{2,12},{3,15},{4,10},{5,9},{6,8},{7,11},{8,6},{9,5},... | collective-permute-start | bytes 393224 | tf_op jit(solution)/shard_map/ppermute | solution.py:68
  15.1 10.1 %collective-permute-start.7 = (bf16[8,4096]{1,0:T(8,128)(2,1)}, bf16[8,4096]{1,0:T(8,128)(2,1)S(1)}, u32[]{:S(2)}, u32[]{:S(2)}) collective-permute-start(bf16[8,4096]{1,0:T(8,128)(2,1)} %attention.1), channel_id=1, source_target_pairs={{0,2},{1,3},{2,0},{3,1},{4,6},{5,7},{6,4},{7,5},{8,10},{9,11},{10,... | collective-permute-start | bytes 196616 | tf_op jit(solution)/shard_map/ppermute | solution.py:63
  16.8 11.9 %collective-permute-start.6 = (bf16[16,4096]{1,0:T(8,128)(2,1)S(1)}, bf16[16,4096]{1,0:T(8,128)(2,1)S(1)}, u32[]{:S(2)}, u32[]{:S(2)}) collective-permute-start(bf16[16,4096]{1,0:T(8,128)(2,1)S(1)} %collective-permute-done.3.refs_3_), channel_id=1, source_target_pairs={{0,1},{1,0},{2,3},{3,2},{4,5},{5,4},{6,7},{7,6},{8,9},{9,8},{10,11... | collective-permute-start | bytes 393224 | tf_op jit(solution)/shard_map/ppermute | solution.py:60
  24.6 4.1 %collective-permute-start.5 = (bf16[16,4096]{1,0:T(8,128)(2,1)S(1)}, bf16[16,4096]{1,0:T(8,128)(2,1)S(1)}, u32[]{:S(2)}, u32[]{:S(2)}) collective-permute-start(bf16[16,4096]{1,0:T(8,128)(2,1)S(1)} %collective-permute-done.2.refs_2_), channel_id=1, source_target_pairs={{0,1},{1,0},{2,3},{3,2},{4,5},{5,4},{6,7},{7,6},{8,9},{9,8},{10,11... | collective-permute-start | bytes 393224 | tf_op jit(solution)/shard_map/ppermute | solution.py:60
  24.6 4.1 %collective-permute-start.4 = (bf16[16,4096]{1,0:T(8,128)(2,1)S(1)}, bf16[16,4096]{1,0:T(8,128)(2,1)S(1)}, u32[]{:S(2)}, u32[]{:S(2)}) collective-permute-start(bf16[16,4096]{1,0:T(8,128)(2,1)S(1)} %collective-permute-done.1.refs_1_), channel_id=1, source_target_pairs={{0,1},{1,0},{2,3},{3,2},{4,5},{5,4},{6,7},{7,6},{8,9},{9,8},{10,11... | collective-permute-start | bytes 393224 | tf_op jit(solution)/shard_map/ppermute | solution.py:60
  25.1 3.6 %collective-permute-start.8 = (bf16[8,4096]{1,0:T(8,128)(2,1)S(1)}, bf16[8,4096]{1,0:T(8,128)(2,1)S(1)}, u32[]{:S(2)}, u32[]{:S(2)}) collective-permute-start(bf16[8,4096]{1,0:T(8,128)(2,1)S(1)} %collective-permute-done.7.refs_7_), channel_id=1, source_target_pairs={{0,1},{1,0},{2,3},{3,2},{4,5},{5,4},{6,7},{7,6},{8,9},{9,8},{10,11... | collective-permute-start | bytes 196616 | tf_op jit(solution)/shard_map/ppermute | solution.py:60
  30.4 1.4 %collective-permute-start.9 = (bf16[256,128]{1,0:T(8,128)(2,1)S(1)}, bf16[256,128]{1,0:T(8,128)(2,1)S(1)}, u32[]{:S(2)}, u32[]{:S(2)}) collective-permute-start(bf16[256,128]{1,0:T(8,128)(2,1)S(1)} %projection.1.mine_ref.stream_ref), channel_id=1, source_target_pairs={{0,1},{1,0},{2,3},{3,2},{4,5},{5,4},{6,7},{7,6},{8,9},{9,8},{10,11... | collective-permute-start | bytes 196616 | tf_op jit(solution)/shard_map/ppermute | solution.py:60
  31.8 7.4 %collective-permute-start.12 = (bf16[512,128]{1,0:T(8,128)(2,1)S(1)}, bf16[512,128]{1,0:T(8,128)(2,1)S(1)}, u32[]{:S(2)}, u32[]{:S(2)}) collective-permute-start(bf16[512,128]{1,0:T(8,128)(2,1)S(1)} %pair.1.refs_0_), channel_id=1, source_target_pairs={{0,6},{1,5},{2,4},{3,7},{4,2},{5,1},{6,0},{7,3},{8,14},{9,13},{10,... | collective-permute-start | bytes 393224 | tf_op jit(solution)/shard_map/ppermute | solution.py:68
  33.6 13.2 %collective-permute-start.11 = (bf16[512,128]{1,0:T(8,128)(2,1)S(1)}, bf16[512,128]{1,0:T(8,128)(2,1)S(1)}, u32[]{:S(2)}, u32[]{:S(2)}) collective-permute-start(bf16[512,128]{1,0:T(8,128)(2,1)S(1)} %pair.1.refs_0_), channel_id=1, source_target_pairs={{0,10},{1,9},{2,8},{3,11},{4,14},{5,13},{6,12},{7,15},{8,2},{9,1},... | collective-permute-start | bytes 393224 | tf_op jit(solution)/shard_map/ppermute | solution.py:68
  35.8 11.0 %collective-permute-start.10 = (bf16[512,128]{1,0:T(8,128)(2,1)S(1)}, bf16[512,128]{1,0:T(8,128)(2,1)S(1)}, u32[]{:S(2)}, u32[]{:S(2)}) collective-permute-start(bf16[512,128]{1,0:T(8,128)(2,1)S(1)} %pair.1.refs_0_), channel_id=1, source_target_pairs={{0,14},{1,13},{2,12},{3,15},{4,10},{5,9},{6,8},{7,11},{8,6},{9,5},... | collective-permute-start | bytes 393224 | tf_op jit(solution)/shard_map/ppermute | solution.py:68
  37.1 10.3 %collective-permute-start.16 = (bf16[256,128]{1,0:T(8,128)(2,1)S(1)}, bf16[256,128]{1,0:T(8,128)(2,1)S(1)}, u32[]{:S(2)}, u32[]{:S(2)}) collective-permute-start(bf16[256,128]{1,0:T(8,128)(2,1)S(1)} %projection.1.mine_ref.stream_ref), channel_id=1, source_target_pairs={{0,2},{1,3},{2,0},{3,1},{4,6},{5,7},{6,4},{7,5},{8,10},{9,11},{10,... | collective-permute-start | bytes 196616 | tf_op jit(solution)/shard_map/ppermute | solution.py:63
  39.2 11.7 %collective-permute-start.15 = (bf16[512,128]{1,0:T(8,128)(2,1)S(1)}, bf16[512,128]{1,0:T(8,128)(2,1)S(1)}, u32[]{:S(2)}, u32[]{:S(2)}) collective-permute-start(bf16[512,128]{1,0:T(8,128)(2,1)S(1)} %collective-permute-done.12.refs_3_), channel_id=1, source_target_pairs={{0,1},{1,0},{2,3},{3,2},{4,5},{5,4},{6,7},{7,6},{8,9},{9,8},{10,11... | collective-permute-start | bytes 393224 | tf_op jit(solution)/shard_map/ppermute | solution.py:60
  46.8 4.1 %collective-permute-start.14 = (bf16[512,128]{1,0:T(8,128)(2,1)S(1)}, bf16[512,128]{1,0:T(8,128)(2,1)S(1)}, u32[]{:S(2)}, u32[]{:S(2)}) collective-permute-start(bf16[512,128]{1,0:T(8,128)(2,1)S(1)} %collective-permute-done.11.refs_2_), channel_id=1, source_target_pairs={{0,1},{1,0},{2,3},{3,2},{4,5},{5,4},{6,7},{7,6},{8,9},{9,8},{10,11... | collective-permute-start | bytes 393224 | tf_op jit(solution)/shard_map/ppermute | solution.py:60
  46.8 4.1 %collective-permute-start.13 = (bf16[512,128]{1,0:T(8,128)(2,1)S(1)}, bf16[512,128]{1,0:T(8,128)(2,1)S(1)}, u32[]{:S(2)}, u32[]{:S(2)}) collective-permute-start(bf16[512,128]{1,0:T(8,128)(2,1)S(1)} %collective-permute-done.10.refs_1_), channel_id=1, source_target_pairs={{0,1},{1,0},{2,3},{3,2},{4,5},{5,4},{6,7},{7,6},{8,9},{9,8},{10,11... | collective-permute-start | bytes 393224 | tf_op jit(solution)/shard_map/ppermute | solution.py:60
  47.3 3.6 %collective-permute-start.17 = (bf16[256,128]{1,0:T(8,128)(2,1)S(1)}, bf16[256,128]{1,0:T(8,128)(2,1)S(1)}, u32[]{:S(2)}, u32[]{:S(2)}) collective-permute-start(bf16[256,128]{1,0:T(8,128)(2,1)S(1)} %collective-permute-done.16.refs_7_), channel_id=1, source_target_pairs={{0,1},{1,0},{2,3},{3,2},{4,5},{5,4},{6,7},{7,6},{8,9},{9,8},{10,11... | collective-permute-start | bytes 196616 | tf_op jit(solution)/shard_map/ppermute | solution.py:60
  64.8 2.3 %collective-permute-start.18 = (bf16[5,128,512]{2,1,0:T(8,128)(2,1)S(1)}, bf16[5,128,512]{2,1,0:T(8,128)(2,1)S(1)}, u32[]{:S(2)}, u32[]{:S(2)}) collective-permute-start(bf16[5,128,512]{2,1,0:T(8,128)(2,1)S(1)} %theirs.1.own_ref), channel_id=1, source_target_pairs={{0,1},{1,0},{2,3},{3,2},{4,5},{5,4},{6,7},{7,6},{8,9},{9,8},{10,11... | collective-permute-start | bytes 1966088 | tf_op jit(solution)/shard_map/ppermute | solution.py:60
  68.1 9.2 %collective-permute-start.20 = (bf16[128,512]{1,0:T(8,128)(2,1)S(1)}, bf16[128,512]{1,0:T(8,128)(2,1)S(1)}, u32[]{:S(2)}, u32[]{:S(2)}) collective-permute-start(bf16[128,512]{1,0:T(8,128)(2,1)S(1)} %get-tuple-element.28), channel_id=1, source_target_pairs={{0,14},{1,13},{2,12},{3,15},{4,10},{5,9},{6,8},{7,11},{8,6},{9,5},... | collective-permute-start | bytes 393224 | tf_op jit(solution)/shard_map/ppermute | solution.py:68
  71.4 12.9 %collective-permute-start.21 = (bf16[128,512]{1,0:T(8,128)(2,1)S(1)}, bf16[128,512]{1,0:T(8,128)(2,1)S(1)}, u32[]{:S(2)}, u32[]{:S(2)}) collective-permute-start(bf16[128,512]{1,0:T(8,128)(2,1)S(1)} %get-tuple-element.29), channel_id=1, source_target_pairs={{0,10},{1,9},{2,8},{3,11},{4,14},{5,13},{6,12},{7,15},{8,2},{9,1},... | collective-permute-start | bytes 393224 | tf_op jit(solution)/shard_map/ppermute | solution.py:68
  72.3 12.1 %collective-permute-start.22 = (bf16[128,512]{1,0:T(8,128)(2,1)S(1)}, bf16[128,512]{1,0:T(8,128)(2,1)S(1)}, u32[]{:S(2)}, u32[]{:S(2)}) collective-permute-start(bf16[128,512]{1,0:T(8,128)(2,1)S(1)} %get-tuple-element.30), channel_id=1, source_target_pairs={{0,6},{1,5},{2,4},{3,7},{4,2},{5,1},{6,0},{7,3},{8,14},{9,13},{10,... | collective-permute-start | bytes 393224 | tf_op jit(solution)/shard_map/ppermute | solution.py:68
  74.3 10.2 %collective-permute-start.19 = (bf16[128,256]{1,0:T(8,128)(2,1)S(1)}, bf16[128,256]{1,0:T(8,128)(2,1)S(1)}, u32[]{:S(2)}, u32[]{:S(2)}) collective-permute-start(bf16[128,256]{1,0:T(8,128)(2,1)S(1)} %get-tuple-element.27), channel_id=1, source_target_pairs={{0,2},{1,3},{2,0},{3,1},{4,6},{5,7},{6,4},{7,5},{8,10},{9,11},{10,... | collective-permute-start | bytes 196616 | tf_op jit(solution)/shard_map/ppermute | solution.py:63
  84.4 1.3 %collective-permute-start.23 = (bf16[128,256]{1,0:T(8,128)(2,1)S(1)}, bf16[128,256]{1,0:T(8,128)(2,1)S(1)}, u32[]{:S(2)}, u32[]{:S(2)}) collective-permute-start(bf16[128,256]{1,0:T(8,128)(2,1)S(1)} %handover.1), channel_id=1, source_target_pairs={{0,1},{1,0},{2,3},{3,2},{4,5},{5,4},{6,7},{7,6},{8,9},{9,8},{10,11... | collective-permute-start | bytes 196616 | tf_op jit(solution)/shard_map/ppermute | solution.py:60
